TPU v7x, 256 devices: a whole 4x4x8 slice. The times are simulated.
256 devices in a mesh: space: 32 (over z, x), tm: 8 (over y, core).
Axes of the slice: x: 4, y: 4, z: 8, core: 2. Of those that a mesh axis runs over, the one named last changes fastest.
Arguments:
- iterate: float32 [8, 240, 23040], P(None, 'tm', 'space'), may hold values from -6 to 6
- residual: float32 [8, 240, 23040], P(None, 'tm', 'space'), may hold values from -24 to 24
- direction: float32 [8, 240, 23040], P(None, 'tm', 'space'), may hold values from -24 to 24
- diffusivity: float32 [23040], P('space'), may hold values from 0.1 to 0.34
- temporal_factor: float32 [240, 240], replicated, may hold values from 0 to 4
- block_tile: int32 [8, 256], P('tm', 'space'), may hold values from -1 to 479, as said below
- footprints: bfloat16 [8, 256, 64, 1440], P('tm', 'space'), may hold values from -0.15625 to 0.15625
- obs_weight: float32 [8, 32, 64], P('tm', 'space'), may hold values from 0.3 to 3
Outputs:
- iterate_next: float32 [8, 240, 23040], P(None, 'tm', 'space')
- residual_next: float32 [8, 240, 23040], P(None, 'tm', 'space')
- direction_next: float32 [8, 240, 23040], P(None, 'tm', 'space')
Inputs may be any that keep to these rules, and one draw needn't show every extreme that they name: `block_tile`: entry -1 marks a padding slot. Tile g belongs to index g // 15 of space. The valid entries of one device name distinct tiles, at most 2 of them of one owner; in each row of tm one owner is named exactly 2 times by every device.
All inputs are finite; a program needn't handle non-finite values.
Results may differ from a plain program's by a relative error of at most 0.017.
Values may be sent and summed in bfloat16 or wider, within the bound.
No kernel may reach another device: no remote copies, remote signals or barrier semaphores. Data moves between devices by JAX's collectives and lax.ppermute only.
A program may use at most 128 MiB of HBM per device.

v0:
```python
import jax
import jax.numpy as jnp
from jax import lax
from jax.sharding import PartitionSpec as P

LON = 720
TC = 48
NB = 8
DIFF = 2


def for_sending(value):

    def short(part):
        return part.astype(jnp.bfloat16) if part.dtype == jnp.float32 else part

    return jax.tree.map(short, value)


def extended_2(cells, sides, width):
    for axis, dim in sides:
        count = lax.axis_size(axis)
        ends = count - 1
        head = lax.slice_in_dim(cells, 0, width, axis=dim)
        tail = lax.slice_in_dim(cells, cells.shape[dim] - width, cells.shape[dim], axis=dim)
        cells = jnp.concatenate(
            [
                lax.ppermute(tail, axis, [(i, (i + 1) % count) for i in range(ends)]),
                cells,
                lax.ppermute(head, axis, [((i + 1) % count, i) for i in range(ends)]),
            ],
            axis=dim,
        )
    return cells


def temporal(field, matrix):
    combined = jnp.einsum(
        "tu,kuc->ktc",
        matrix,
        lax.all_to_all(
            field.astype(jnp.bfloat16), "tm", split_axis=2, concat_axis=1, tiled=True
        ).astype(field.dtype),
        precision=lax.Precision.HIGHEST,
    )
    return lax.all_to_all(
        for_sending(combined), "tm", split_axis=1, concat_axis=2, tiled=True
    ).astype(combined.dtype)


def diffuse(field, conduct):
    samples, window, cell_count = field.shape
    rows_here = cell_count // LON
    for sweep_index in range(DIFF):
        scaled_field = field * conduct
        extended = extended_2(for_sending(scaled_field), (("space", 2),), LON).astype(
            scaled_field.dtype
        )
        planes = extended.reshape(samples, window, rows_here + 2, LON)
        centre = planes[:, :, 1:-1, :]
        laplace = (
            planes[:, :, :-2, :]
            + planes[:, :, 2:, :]
            + jnp.roll(centre, 1, 3)
            + jnp.roll(centre, -1, 3)
            - 4.0 * centre
        )
        field = field + conduct * laplace.reshape(samples, window, cell_count)
    return field


def local(
    iterate, residual, direction, diffusivity, temporal_factor, block_tile, footprints, obs_weight
):
    samples, window, cell_count = direction.shape
    tiles_here = cell_count // TC
    entries = block_tile[0]
    blocks_here = entries.shape[0]
    present = entries >= 0
    mixed = temporal(direction, temporal_factor)
    spread = diffuse(mixed, diffusivity)
    tiled = spread.astype(jnp.bfloat16).reshape(samples, window, tiles_here, TC)
    empty_blocks = jnp.zeros((blocks_here, samples, window * TC), jnp.float32)
    segment = lax.all_gather(tiled, "space", axis=2, tiled=True)
    count_tiles = segment.shape[2]
    selector = (entries[:, None] == jnp.arange(count_tiles)[None, :]).astype(jnp.bfloat16)
    picked = jnp.einsum("bj,ktjc->bktc", selector, segment, preferred_element_type=jnp.float32)
    blocks = picked.reshape(empty_blocks.shape).astype(jnp.bfloat16)
    footprint = footprints[0]
    batches = obs_weight.shape[1]
    slot_obs = jnp.einsum("bmx,bkx->bkm", footprint, blocks, preferred_element_type=jnp.float32)
    batch_obs = jnp.sum(slot_obs.reshape(batches, NB, samples, footprint.shape[1]), axis=1)
    weighted = (obs_weight[0][:, None, :] * batch_obs).astype(jnp.bfloat16)
    grouped = footprint.reshape(batches, NB, footprint.shape[1], footprint.shape[2])
    gradient = jnp.einsum("anmx,akm->ankx", grouped, weighted, preferred_element_type=jnp.float32)
    gradient = gradient.reshape(blocks_here, samples, footprint.shape[2])
    gradient = jnp.where(present[:, None, None], gradient, 0.0).astype(jnp.bfloat16)
    selector = (
        entries[:, None] == jnp.arange(lax.axis_size("space") * tiles_here)[None, :]
    ).astype(jnp.bfloat16)
    summed = lax.psum_scatter(
        jnp.einsum("bj,bkx->jkx", selector, gradient, preferred_element_type=jnp.float32).astype(
            jnp.bfloat16
        ),
        "space",
        scatter_dimension=0,
        tiled=True,
    ).astype(jnp.float32)
    pulled = (
        summed.reshape(tiles_here, samples, window, TC)
        .transpose(1, 2, 0, 3)
        .reshape(samples, window, cell_count)
    )
    back = diffuse(pulled, diffusivity)
    image = direction + temporal(back, temporal_factor.T)
    old_norm, curvature = lax.psum(
        (jnp.sum(residual * residual, axis=(1, 2)), jnp.sum(direction * image, axis=(1, 2))),
        ("space", "tm"),
    )
    step_size = old_norm / curvature
    residual_next = residual - step_size[:, None, None] * image
    new_norm = lax.psum(jnp.sum(residual_next * residual_next, axis=(1, 2)), ("space", "tm"))
    iterate_next = iterate + step_size[:, None, None] * direction
    direction_next = residual_next + (new_norm / old_norm)[:, None, None] * direction
    return (iterate_next, residual_next, direction_next)


def solution(mesh):
    return jax.shard_map(
        local,
        mesh=mesh,
        in_specs=(
            P(None, "tm", "space"),
            P(None, "tm", "space"),
            P(None, "tm", "space"),
            P("space"),
            P(),
            P("tm", "space"),
            P("tm", "space", None, None),
            P("tm", "space", None),
        ),
        out_specs=(P(None, "tm", "space"), P(None, "tm", "space"), P(None, "tm", "space")),
        check_vma=False,
    )
```

profile of v0, /device:TPU:1, one launch (start us, length us, event | category | flops | bytes accessed | tf_op | source)
XLA Modules:
  0.0 833.4 jit_solution(11026537258770947451)
XLA Ops:
  10.0 2.0 reshape.151
  12.0 14.0 %all_to_all.54 = bf16[8,2,10800]{2,1,0:T(2,128)(2,1)} all-to-all(bf16[8,2,10800]{2,1,0:T(2,128)(2,1)S(1)} %reshape.151), channel_id=1, replica_groups=mesh['space'=32,'tm'=8] {'tm'}, dimensions={0} | all-to-all | bytes 691200 | tf_op jit(solution)/shard_map/all_to_all | solution.py:41
  26.0 3.1 reshape.152
  32.1 12.3 %all_to_all.55 = bf16[8,240,90]{2,0,1:T(8,128)(2,1)S(1)} all-to-all(bf16[8,240,90]{2,0,1:T(8,128)(2,1)S(1)} %copy.98), channel_id=1, replica_groups=mesh['space'=32,'tm'=8] {'tm'}, dimensions={1} | all-to-all | bytes 691200 | tf_op jit(solution)/shard_map/all_to_all | solution.py:46
  46.0 1.9 multiply_convert_fusion.6
  47.9 3.4 collective-permute-start
  54.9 2.8 collective-permute-done
  57.7 4.6 collective-permute-done.1
  67.5 3.1 collective-permute-start.2
  73.5 2.7 reshape.137
  76.2 3.1 reshape.128
  84.3 3.1 reshape.130
  87.4 4.9 fusion.5
  93.8 215.8 %all-gather.2.cloned.1.call-done = bf16[8,30,480,48]{3,0,1,2:T(8,128)(2,1)} async-done(((bf16[8,30,15,48]{3,0,1,2:T(8,128)(2,1)}), bf16[8,30,480,48]{3,0,1,2:T(8,128)(2,1)}) %all-gather.2.cloned.1.call-update) | async-done | bytes 11059216 | tf_op jit(solution)/shard_map/all_gather | solution.py:84
  309.6 26.4 %fusion.9 = bf16[8,8,30,48]{3,0,2,1:T(8,128)(2,1)S(1)} fusion(bf16[8,30,480,48]{3,0,1,2:T(8,128)(2,1)} %all-gather.2.cloned.1.call-done, s32[8]{0:T(128)S(1)} %bitcast.153), kind=kOutput, calls=%fused_computation.14 | convolution fusion | flops 88569600 | bytes 11243552 | tf_op jit(solution)/shard_map/bj,ktjc->bktc/dot_general | solution.py:87
  338.1 3.7 convolution_convert_fusion
  341.8 20.4 %copy.109 = bf16[480,8,1440]{2,1,0:T(8,128)(2,1)} copy(bf16[480,8,1440]{2,0,1:T(8,128)(2,1)S(1)} %convolution_convert_fusion) | data formatting | bytes 22118400 | tf_op jit(solution)/shard_map/convert_element_type | solution.py:102
  362.2 230.0 %reduce-scatter.2.cloned.1.call-done = bf16[15,8,1440]{2,1,0:T(8,128)(2,1)} async-done(((bf16[480,8,1440]{2,1,0:T(8,128)(2,1)}), bf16[15,8,1440]{2,1,0:T(8,128)(2,1)}) %reduce-scatter.2.cloned.1.call-update) | async-done | bytes 345616 | tf_op jit(solution)/shard_map/reduce_scatter | solution.py:101
  592.2 3.0 reshape.141
  595.3 2.6 copy.110
  599.5 3.0 collective-permute-start.4
  604.7 1.8 collective-permute-done.4
  606.5 4.6 collective-permute-done.5
  614.2 2.7 collective-permute-start.6
  618.4 2.9 collective-permute-done.6
  621.4 3.8 collective-permute-done.7
  627.8 2.0 reshape.153
  629.8 19.2 %all_to_all.56 = bf16[8,2,10800]{2,1,0:T(2,128)(2,1)S(1)} all-to-all(bf16[8,2,10800]{2,1,0:T(2,128)(2,1)S(1)} %reshape.153), channel_id=1, replica_groups=mesh['space'=32,'tm'=8] {'tm'}, dimensions={0} | all-to-all | bytes 691200 | tf_op jit(solution)/shard_map/all_to_all | solution.py:41
  652.8 12.3 %all_to_all.57 = bf16[8,240,90]{2,0,1:T(8,128)(2,1)S(1)} all-to-all(bf16[8,240,90]{2,0,1:T(8,128)(2,1)S(1)} %copy.116), channel_id=1, replica_groups=mesh['space'=32,'tm'=8] {'tm'}, dimensions={1} | all-to-all | bytes 691200 | tf_op jit(solution)/shard_map/all_to_all | solution.py:46
  667.8 81.2 %all-reduce = (f32[8]{0:T(128)S(1)}, f32[8]{0:T(128)S(1)}) all-reduce(f32[8]{0:T(128)S(1)} %get-tuple-element.31, f32[8]{0:T(128)S(1)} %get-tuple-element.7), channel_id=1, replica_groups=mesh['space'=32,'tm'=8] {'space','tm'}, use_global_device_ids=true, to_apply=%region_1.2 | all-reduce | flops 16 | bytes 128 | tf_op jit(solution)/shard_map/psum | solution.py:116
  750.5 73.2 %psum.23 = f32[8]{0:T(128)S(1)} all-reduce(f32[8]{0:T(128)S(1)} %get-tuple-element.5), channel_id=1, replica_groups=mesh['space'=32,'tm'=8] {'space','tm'}, use_global_device_ids=true, to_apply=%region_6.7 | all-reduce | flops 8 | bytes 64 | tf_op jit(solution)/shard_map/psum | solution.py:122
  823.8 2.5 multiply_add_fusion
  (89 shorter events, 46.5 us)
Async XLA Ops:
  7.2 329.7 %copy-start = (bf16[1,8,64,1440]{3,2,1,0:T(8,128)(2,1)S(1)}, bf16[1,8,64,1440]{3,2,1,0:T(8,128)(2,1)}, u32[]{:S(2)}) copy-start(bf16[1,8,64,1440]{3,2,1,0:T(8,128)(2,1)} %param.14) | copy-start | bytes 4423684
  7.2 302.4 %all-gather.2.cloned.1.call-start = ((), (), s32[]{:S(2)}) async-start(), calls=%async_computation.5 | async-start | bytes 30412800 | tf_op jit(solution)/shard_map/all_gather | solution.py:84
  44.4 1.5 copy-start.11
  47.9 9.9 %collective-permute-start = (bf16[8,30,720]{2,0,1:T(8,128)(2,1)}, bf16[8,30,720]{2,0,1:T(8,128)(2,1)}, u32[]{:S(2)}, u32[]{:S(2)}) collective-permute-start(bf16[8,30,720]{2,0,1:T(8,128)(2,1)} %multiply_convert_fusion.6), channel_id=1, source_target_pairs={{0,8},{8,16},{16,24},{24,32},{32,40},{40,48},{48,56},{56,64},{64,7... | collective-permute-start | bytes 1036808 | tf_op jit(solution)/shard_map/ppermute | solution.py:28
  51.3 11.0 %collective-permute-start.1 = (bf16[8,30,720]{2,0,1:T(8,128)(2,1)}, bf16[8,30,720]{2,0,1:T(8,128)(2,1)}, u32[]{:S(2)}, u32[]{:S(2)}) collective-permute-start(bf16[8,30,720]{2,0,1:T(8,128)(2,1)} %multiply_convert_fusion.6), channel_id=1, source_target_pairs={{8,0},{16,8},{24,16},{32,24},{40,32},{48,40},{56,48},{64,56},{72,6... | collective-permute-start | bytes 1036808 | tf_op jit(solution)/shard_map/ppermute | solution.py:30
  63.6 1.1 copy-start.3
  64.7 2.0 copy-start.6
  65.8 0.9 copy-start.2
  67.5 11.8 %collective-permute-start.2 = (bf16[8,30,720]{2,0,1:T(8,128)(2,1)}, bf16[8,30,720]{2,0,1:T(8,128)(2,1)}, u32[]{:S(2)}, u32[]{:S(2)}) collective-permute-start(bf16[8,30,720]{2,0,1:T(8,128)(2,1)} %fusion.47), channel_id=1, source_target_pairs={{0,8},{8,16},{16,24},{24,32},{32,40},{40,48},{48,56},{56,64},{64,7... | collective-permute-start | bytes 1036808 | tf_op jit(solution)/shard_map/ppermute | solution.py:28
  70.7 9.8 %collective-permute-start.3 = (bf16[8,30,720]{2,0,1:T(8,128)(2,1)}, bf16[8,30,720]{2,0,1:T(8,128)(2,1)}, u32[]{:S(2)}, u32[]{:S(2)}) collective-permute-start(bf16[8,30,720]{2,0,1:T(8,128)(2,1)} %fusion.47), channel_id=1, source_target_pairs={{8,0},{16,8},{24,16},{32,24},{40,32},{48,40},{56,48},{64,56},{72,6... | collective-permute-start | bytes 1036808 | tf_op jit(solution)/shard_map/ppermute | solution.py:30
  92.3 1.4 copy-start.12
  93.5 498.7 %reduce-scatter.2.cloned.1.call-start = ((), (), s32[]{:S(2)}) async-start(), calls=%async_computation.6 | async-start | bytes 12165120 | tf_op jit(solution)/shard_map/reduce_scatter | solution.py:101
  309.6 27.3 %copy-start.13 = (f32[1,1,64]{2,1,0:T(1,128)S(1)}, f32[1,1,64]{2,1,0:T(1,128)}, u32[]{:S(2)}) copy-start(f32[1,1,64]{2,1,0:T(1,128)} %param.15) | copy-start | bytes 772
  599.5 7.0 collective-permute-start.4
  602.5 8.6 %collective-permute-start.5 = (bf16[8,30,720]{2,0,1:T(8,128)(2,1)}, bf16[8,30,720]{2,0,1:T(8,128)(2,1)}, u32[]{:S(2)}, u32[]{:S(2)}) collective-permute-start(bf16[8,30,720]{2,0,1:T(8,128)(2,1)} %multiply_convert_fusion.3), channel_id=1, source_target_pairs={{8,0},{16,8},{24,16},{32,24},{40,32},{48,40},{56,48},{64,56},{72,6... | collective-permute-start | bytes 1036808 | tf_op jit(solution)/shard_map/ppermute | solution.py:30
  604.7 7.7 copy-start.4
  612.5 1.1 copy-start.5
  614.2 7.1 collective-permute-start.6
  616.9 8.3 collective-permute-start.7
  649.0 2.9 copy-start.10
  665.1 1.1 copy-start.7
  665.5 1.2 copy-start.8
  750.5 75.8 %copy-start.9 = (f32[8,30,720]{2,0,1:T(8,128)}, f32[8,30,720]{2,0,1:T(8,128)S(1)}, u32[]{:S(2)}) copy-start(f32[8,30,720]{2,0,1:T(8,128)S(1)} %get-tuple-element.6) | copy-start | bytes 2073604
  823.8 2.6 copy-start.1
Sparse Core Ops, SparseCore 0:
  93.6 215.9 all-gather.1
  362.4 229.8 reduce-scatter.1
where the time goes:
time: 841 us; the launch traced here: 833 us
  waiting for transfers between devices  468 us (56%)
  blocking collectives  212 us (25%)
  local copies, waits for them, and re-layouts  62.5 us (7%)
  matrix products  33.5 us (4%)
  other arithmetic  25.1 us (3%)
  starting transfers between devices  18 us (2%)
  between operations  14.6 us (2%)
    reduce_scatter x1, waiting for transfers between devices, local(): lax.psum_scatter(jnp.einsum('bj,bkx->jkx', selector, gradient, preferred_...  230 us
    all_gather x1, waiting for transfers between devices, local(): segment = lax.all_gather(tiled, 'space', axis=2, tiled=True)  216 us
    psum x1, blocking collectives, local(): lax.psum((jnp.sum(residual * residual, axis=(1, 2)), jnp.sum(direction *...  81.2 us
    psum x1, blocking collectives, local(): lax.psum(jnp.sum(residual_next * residual_next, axis=(1, 2)), ('space', '...  73.2 us
    all_to_all x2, blocking collectives, temporal(): lax.all_to_all(field.astype(jnp.bfloat16), 'tm', split_axis=2, concat_axi...  33.1 us
    dot_general x1, matrix products, local(): jnp.einsum('bj,ktjc->bktc', selector, segment, preferred_element_type=jnp...  26.4 us
    all_to_all x2, blocking collectives, temporal(): lax.all_to_all(for_sending(combined), 'tm', split_axis=1, concat_axis=2,...  24.5 us
    convert_element_type x1, local copies, waits for them, and re-layouts, local(): jnp.einsum('bj,bkx->jkx', selector, gradient, preferred_element_type=jnp....  20.4 us
  transfers between devices with their start and end apart: 10, of which 9 were waited for; matrix products, arithmetic and copies ran while one was open for 1% of the time, Pallas kernels for 0%

commit v1 on v0

--- a/solution.py
+++ b/solution.py
@@ -81,7 +81,9 @@
     spread = diffuse(mixed, diffusivity)
     tiled = spread.astype(jnp.bfloat16).reshape(samples, window, tiles_here, TC)
     empty_blocks = jnp.zeros((blocks_here, samples, window * TC), jnp.float32)
-    segment = lax.all_gather(tiled, "space", axis=2, tiled=True)
+    segment = jnp.concatenate(
+        lax.all_to_all(jnp.stack([tiled] * lax.axis_size("space")), "space", 0, 0), axis=2
+    )
     count_tiles = segment.shape[2]
     selector = (entries[:, None] == jnp.arange(count_tiles)[None, :]).astype(jnp.bfloat16)
     picked = jnp.einsum("bj,ktjc->bktc", selector, segment, preferred_element_type=jnp.float32)

time: 841 us -> 1050 us (1.25)
  local copies, waits for them, and re-layouts: 62.5 us -> 238 us
  waiting for transfers between devices: 468 us -> 499 us
  matrix products: 33.5 us -> 15.5 us
  starting transfers between devices: 18 us -> 33.1 us
    all_to_all x0 -> x1, waiting for transfers between devices: none -> 235 us  [local(): lax.all_to_all(jnp.stack([tiled] * lax.axis_size('space')), 'space', 0, 0)]
    all_gather x1 -> x0, waiting for transfers between devices: 216 us -> none  [local(): segment = lax.all_gather(tiled, 'space', axis=2, tiled=True)]
    unnamed x32 -> x29, local copies, waits for them, and re-layouts: 12.3 us -> 116 us
    reshape x0 -> x2, local copies, waits for them, and re-layouts: none -> 40.1 us  [local(): jnp.concatenate(lax.all_to_all(jnp.stack([tiled] * lax.axis_size('space')...]
    dot_general x0 -> x1, local copies, waits for them, and re-layouts: none -> 31.6 us  [local(): jnp.einsum('bj,ktjc->bktc', selector, segment, preferred_element_type=jnp...]
    dot_general x1, matrix products: 26.4 us -> 7.5 us  [local(): jnp.einsum('bj,ktjc->bktc', selector, segment, preferred_element_type=jnp...]
    all_to_all x0 -> x1, starting transfers between devices: none -> 15 us  [local(): lax.all_to_all(jnp.stack([tiled] * lax.axis_size('space')), 'space', 0, 0)]
    reduce_scatter x1, waiting for transfers between devices: 230 us -> 244 us  [local(): lax.psum_scatter(jnp.einsum('bj,bkx->jkx', selector, gradient, preferred_...]
  transfers between devices with their start and end apart: 10 -> 10, of which waited for: 9 -> 8; matrix products, arithmetic and copies ran while one was open for 1% -> 1% of each run, Pallas kernels for 0% -> 0%
where the time goes in v1:
time: 1050 us; the launch traced here: 1040 us
  waiting for transfers between devices  499 us (48%)
  local copies, waits for them, and re-layouts  238 us (23%)
  blocking collectives  212 us (20%)
  starting transfers between devices  33.1 us (3%)
  other arithmetic  29.5 us (3%)
  matrix products  15.5 us (1%)
  between operations  14.6 us (1%)
    reduce_scatter x1, waiting for transfers between devices, local(): lax.psum_scatter(jnp.einsum('bj,bkx->jkx', selector, gradient, preferred_...  244 us
    all_to_all x1, waiting for transfers between devices, local(): lax.all_to_all(jnp.stack([tiled] * lax.axis_size('space')), 'space', 0, 0)  235 us
    unnamed x29, local copies, waits for them, and re-layouts  116 us
    psum x1, blocking collectives, local(): lax.psum((jnp.sum(residual * residual, axis=(1, 2)), jnp.sum(direction *...  81.2 us
    psum x1, blocking collectives, local(): lax.psum(jnp.sum(residual_next * residual_next, axis=(1, 2)), ('space', '...  73.2 us
    reshape x2, local copies, waits for them, and re-layouts, local(): jnp.concatenate(lax.all_to_all(jnp.stack([tiled] * lax.axis_size('space')...  40.1 us
    all_to_all x2, blocking collectives, temporal(): lax.all_to_all(field.astype(jnp.bfloat16), 'tm', split_axis=2, concat_axi...  33.2 us
    dot_general x1, local copies, waits for them, and re-layouts, local(): jnp.einsum('bj,ktjc->bktc', selector, segment, preferred_element_type=jnp...  31.6 us
  transfers between devices with their start and end apart: 10, of which 8 were waited for; matrix products, arithmetic and copies ran while one was open for 1% of the time, Pallas kernels for 0%

profile of v1, /device:TPU:1, one launch (start us, length us, event | category | flops | bytes accessed | tf_op | source)
XLA Modules:
  0.0 1042.3 jit_solution(13317096539624262060)
XLA Ops:
  12.0 14.0 %all_to_all.59 = bf16[8,2,10800]{2,1,0:T(2,128)(2,1)} all-to-all(bf16[8,2,10800]{2,1,0:T(2,128)(2,1)S(1)} %reshape.161), channel_id=1, replica_groups=mesh['space'=32,'tm'=8] {'tm'}, dimensions={0} | all-to-all | bytes 691200 | tf_op jit(solution)/shard_map/all_to_all | solution.py:41
  25.9 3.1 reshape.162
  32.1 12.3 %all_to_all.60 = bf16[8,240,90]{2,0,1:T(8,128)(2,1)S(1)} all-to-all(bf16[8,240,90]{2,0,1:T(8,128)(2,1)S(1)} %copy.99), channel_id=1, replica_groups=mesh['space'=32,'tm'=8] {'tm'}, dimensions={1} | all-to-all | bytes 691200 | tf_op jit(solution)/shard_map/all_to_all | solution.py:46
  47.8 3.4 collective-permute-start
  54.8 2.8 collective-permute-done
  57.7 4.6 collective-permute-done.1
  67.5 3.1 collective-permute-start.2
  76.5 3.1 reshape.137
  84.2 3.1 reshape.139
  87.3 4.9 fusion.3
  92.3 10.0 broadcast_bitcast_fusion
  102.3 50.2 %reshape.163 = bf16[32,2,86400]{2,1,0:T(2,128)(2,1)} reshape(bf16[32,30,15,8,48]{4,3,2,1,0:T(8,128)(2,1)} %broadcast_bitcast_fusion) | data formatting | bytes 22118400
  152.5 15.0 %all-to-all-start.2 = ((bf16[32,2,86400]{2,1,0:T(2,128)(2,1)}), bf16[32,2,86400]{2,1,0:T(2,128)(2,1)}, u32[]{:S(2)}, u32[]{:S(2)}) async-start(bf16[32,2,86400]{2,1,0:T(2,128)(2,1)} %reshape.163), calls=%async_computation.2 | async-start | bytes 22118400 | tf_op jit(solution)/shard_map/all_to_all | solution.py:85
  167.8 235.5 %all-to-all-done.2 = bf16[32,2,86400]{2,1,0:T(2,128)(2,1)} async-done(((bf16[32,2,86400]{2,1,0:T(2,128)(2,1)}), bf16[32,2,86400]{2,1,0:T(2,128)(2,1)}, u32[]{:S(2)}, u32[]{:S(2)}) %all-to-all-start.2) | async-done | bytes 11059232 | tf_op jit(solution)/shard_map/all_to_all | solution.py:85
  403.2 42.2 %reshape.164 = bf16[32,30,15,8,48]{4,3,2,1,0:T(8,128)(2,1)} reshape(bf16[32,2,86400]{2,1,0:T(2,128)(2,1)} %all-to-all-done.2) | data formatting | bytes 22118400
  445.5 20.5 %bitcast_bitcast_fusion = bf16[8,30,32,15,48]{4,0,3,1,2:T(8,128)(2,1)} fusion(bf16[32,30,15,8,48]{4,3,2,1,0:T(8,128)(2,1)} %reshape.164), kind=kLoop, calls=%fused_computation.94 | loop fusion | bytes 22118400 | tf_op jit(solution)/shard_map/reshape | solution.py:84
  466.0 19.6 %copy.106 = bf16[8,30,32,15,48]{4,0,3,2,1:T(8,128)(2,1)} copy(bf16[8,30,32,15,48]{4,0,3,1,2:T(8,128)(2,1)} %bitcast_bitcast_fusion) | data formatting | bytes 22118400 | tf_op jit(solution)/shard_map/reshape | solution.py:84
  485.6 31.6 %copy.107 = bf16[8,30,48,480]{3,2,1,0:T(8,128)(2,1)} copy(bf16[8,30,48,480]{2,0,3,1:T(8,128)(2,1)} %bitcast.146) | data formatting | bytes 22118400 | tf_op jit(solution)/shard_map/bj,ktjc->bktc/dot_general | solution.py:89
  517.2 7.5 convolution_convert_fusion.1
  525.9 3.7 convolution_convert_fusion
  529.6 20.4 %copy.110 = bf16[480,8,1440]{2,1,0:T(8,128)(2,1)} copy(bf16[480,8,1440]{2,0,1:T(8,128)(2,1)S(1)} %convolution_convert_fusion) | data formatting | bytes 22118400 | tf_op jit(solution)/shard_map/convert_element_type | solution.py:104
  550.1 243.6 %reduce-scatter.2.cloned.1.call-done = bf16[15,8,1440]{2,1,0:T(8,128)(2,1)} async-done(((bf16[480,8,1440]{2,1,0:T(8,128)(2,1)}), bf16[15,8,1440]{2,1,0:T(8,128)(2,1)}) %reduce-scatter.2.cloned.1.call-update) | async-done | bytes 345616 | tf_op jit(solution)/shard_map/reduce_scatter | solution.py:103
  793.7 3.2 reshape.152
  803.1 3.1 collective-permute-start.4
  810.4 4.4 collective-permute-done.5
  822.3 3.1 collective-permute-done.6
  825.4 3.8 collective-permute-done.7
  833.8 19.3 %all_to_all.61 = bf16[8,2,10800]{2,1,0:T(2,128)(2,1)} all-to-all(bf16[8,2,10800]{2,1,0:T(2,128)(2,1)S(1)} %reshape.165), channel_id=1, replica_groups=mesh['space'=32,'tm'=8] {'tm'}, dimensions={0} | all-to-all | bytes 691200 | tf_op jit(solution)/shard_map/all_to_all | solution.py:41
  853.1 3.1 reshape.166
  859.2 12.5 %all_to_all.62 = bf16[8,240,90]{2,0,1:T(8,128)(2,1)S(1)} all-to-all(bf16[8,240,90]{2,0,1:T(8,128)(2,1)S(1)} %copy.117), channel_id=1, replica_groups=mesh['space'=32,'tm'=8] {'tm'}, dimensions={1} | all-to-all | bytes 691200 | tf_op jit(solution)/shard_map/all_to_all | solution.py:46
  875.8 81.2 %all-reduce = (f32[8]{0:T(128)S(1)}, f32[8]{0:T(128)S(1)}) all-reduce(f32[8]{0:T(128)S(1)} %get-tuple-element.31, f32[8]{0:T(128)S(1)} %get-tuple-element.7), channel_id=1, replica_groups=mesh['space'=32,'tm'=8] {'space','tm'}, use_global_device_ids=true, to_apply=%region_1.2 | all-reduce | flops 16 | bytes 128 | tf_op jit(solution)/shard_map/psum | solution.py:118
  959.3 73.2 %psum.23 = f32[8]{0:T(128)S(1)} all-reduce(f32[8]{0:T(128)S(1)} %get-tuple-element.5), channel_id=1, replica_groups=mesh['space'=32,'tm'=8] {'space','tm'}, use_global_device_ids=true, to_apply=%region_6.7 | all-reduce | flops 8 | bytes 64 | tf_op jit(solution)/shard_map/psum | solution.py:124
  (85 shorter events, 66.2 us)
Async XLA Ops:
  7.2 517.5 %copy-start = (bf16[1,8,64,1440]{3,2,1,0:T(8,128)(2,1)S(1)}, bf16[1,8,64,1440]{3,2,1,0:T(8,128)(2,1)}, u32[]{:S(2)}) copy-start(bf16[1,8,64,1440]{3,2,1,0:T(8,128)(2,1)} %param.14) | copy-start | bytes 4423684
  44.4 1.5 copy-start.8
  47.8 9.9 collective-permute-start
  51.2 11.0 %collective-permute-start.1 = (bf16[8,30,720]{2,0,1:T(8,128)(2,1)}, bf16[8,30,720]{2,0,1:T(8,128)(2,1)}, u32[]{:S(2)}, u32[]{:S(2)}) collective-permute-start(bf16[8,30,720]{2,0,1:T(8,128)(2,1)} %multiply_convert_fusion.6), channel_id=1, source_target_pairs={{8,0},{16,8},{24,16},{32,24},{40,32},{48,40},{56,48},{64,56},{72,6... | collective-permute-start | bytes 1036808 | tf_op jit(solution)/shard_map/ppermute | solution.py:30
  63.5 1.1 copy-start.3
  64.6 2.0 copy-start.5
  65.8 0.9 copy-start.2
  67.5 12.1 %collective-permute-start.2 = (bf16[8,30,720]{2,0,1:T(8,128)(2,1)}, bf16[8,30,720]{2,0,1:T(8,128)(2,1)}, u32[]{:S(2)}, u32[]{:S(2)}) collective-permute-start(bf16[8,30,720]{2,0,1:T(8,128)(2,1)} %fusion.42), channel_id=1, source_target_pairs={{0,8},{8,16},{16,24},{24,32},{32,40},{40,48},{48,56},{56,64},{64,7... | collective-permute-start | bytes 1036808 | tf_op jit(solution)/shard_map/ppermute | solution.py:28
  70.6 9.8 collective-permute-start.3
  152.5 15.2 %copy-start.9 = (s32[1,8]{1,0:T(1,128)S(1)}, s32[1,8]{1,0:T(1,128)}, u32[]{:S(2)}) copy-start(s32[1,8]{1,0:T(1,128)} %param.13) | copy-start | bytes 100
  152.5 250.7 %all-to-all-start.2 = ((bf16[32,2,86400]{2,1,0:T(2,128)(2,1)}), bf16[32,2,86400]{2,1,0:T(2,128)(2,1)}, u32[]{:S(2)}, u32[]{:S(2)}) async-start(bf16[32,2,86400]{2,1,0:T(2,128)(2,1)} %reshape.163), calls=%async_computation.2 | async-start | bytes 22118400 | tf_op jit(solution)/shard_map/all_to_all | solution.py:85
  167.5 626.2 %reduce-scatter.2.cloned.1.call-start = ((), (), s32[]{:S(2)}) async-start(), calls=%async_computation.6 | async-start | bytes 12165120 | tf_op jit(solution)/shard_map/reduce_scatter | solution.py:103
  517.2 7.5 copy-start.10
  803.1 7.2 collective-permute-start.4
  806.2 8.6 collective-permute-start.5
  816.1 1.1 copy-start.4
  817.2 1.1 copy-start.1
  818.4 7.0 collective-permute-start.6
  821.0 8.3 collective-permute-start.7
  871.8 1.5 copy-start.6
  873.3 83.8 %copy-start.7 = (f32[8,30,720]{2,0,1:T(8,128)S(1)}, f32[8,30,720]{2,0,1:T(8,128)}, u32[]{:S(2)}) copy-start(f32[8,30,720]{2,0,1:T(8,128)} %param.9) | copy-start | bytes 2073604
Sparse Core Ops, SparseCore 0:
  550.2 243.4 reduce-scatter.1
